TPU v7x, 256 devices: a whole 4x4x8 slice. The times are simulated.
256 devices in a mesh: dp: 16 (over z, y_lo), tensor: 4 (over x), section: 4 (over y_hi, core).
Axes of the slice: x: 4, y: 4 (y_hi: 2, y_lo: 2; y = y_hi * 2 + y_lo), z: 8, core: 2. Of those that a mesh axis runs over, the one named last changes fastest.
Arguments:
- grad_parts: bfloat16 [4, 16, 4, 1024, 1024], P('section', 'dp', None, None, 'tensor'), may hold values from -1.5 to 1.5
- first_moment: float32 [4, 4, 1024, 1024], P('section', 'tensor', 'dp'), may hold values from -3 to 3
- second_moment: float32 [4, 4, 1024, 1024], P('section', 'tensor', 'dp'), may hold values from 0.1 to 4
- left_stat: float32 [4, 4, 1024, 1024], P('section', 'tensor', 'dp'), may hold values from -12288 to 184320
- right_stat: float32 [4, 4, 1024, 1024], P('section', 'tensor', 'dp'), may hold values from -12288 to 184320
- left_basis: float32 [4, 4, 1024, 1024], P('section', 'tensor', 'dp'), may hold values from -0.1875 to 0.1875
- right_basis: float32 [4, 4, 1024, 1024], P('section', 'tensor', 'dp'), may hold values from -0.1875 to 0.1875
- gain_grads: float32 [4, 16, 4, 2, 1024], P('section', 'dp', 'tensor'), may hold values from -1.2 to 1.2
- gain_first: float32 [4, 2, 1024], P('section'), may hold values from -3 to 3
- gain_second: float32 [4, 2, 1024], P('section'), may hold values from 0.1 to 4
- table_grads: float32 [4, 16, 32, 16], P('section', 'dp', None, 'tensor'), may hold values from -1.2 to 1.2
- table_first: float32 [32, 16], P(None, 'tensor'), may hold values from -3 to 3
- table_second: float32 [32, 16], P(None, 'tensor'), may hold values from 0.1 to 4
Outputs:
- update: float32 [4, 4, 1024, 1024], P('section', 'tensor', 'dp')
- first_next: float32 [4, 4, 1024, 1024], P('section', 'tensor', 'dp')
- second_next: float32 [4, 4, 1024, 1024], P('section', 'tensor', 'dp')
- left_next: float32 [4, 4, 1024, 1024], P('section', 'tensor', 'dp')
- right_next: float32 [4, 4, 1024, 1024], P('section', 'tensor', 'dp')
- left_rotation: float32 [4, 4, 1024, 1024], P('section', 'tensor', 'dp')
- right_rotation: float32 [4, 4, 1024, 1024], P('section', 'tensor', 'dp')
- gain_update: float32 [4, 2, 1024], P('section')
- gain_moment: float32 [4, 2, 1024], P('section')
- gain_squares: float32 [4, 2, 1024], P('section')
- table_update: float32 [32, 16], P(None, 'tensor')
- table_moment: float32 [32, 16], P(None, 'tensor')
- table_squares: float32 [32, 16], P(None, 'tensor')
All inputs are finite; a program needn't handle non-finite values.
Results may differ from a plain program's by a relative error of at most 0.014.
Values may be sent and summed in bfloat16 or wider, within the bound.
A program may use at most 64 MiB of HBM per device.

v0:
```python
import jax
import jax.numpy as jnp
from jax import lax
from jax.sharding import PartitionSpec as P

NS_ITERS = 3
beta_first = 0.9
beta_second = 0.95
beta_stat = 0.95
adam_eps = 1e-08
norm_eps = 1e-06
step_count = 10.0


def to_half(value):
    return value.astype(jnp.bfloat16)


def batched(pattern, left, right):
    return jnp.einsum(pattern, left, right, preferred_element_type=jnp.float32)


def adam_direction(first, second):
    first_hat = first / (1.0 - beta_first**step_count)
    second_hat = second / (1.0 - beta_second**step_count)
    return first_hat / (jnp.sqrt(second_hat) + adam_eps)


def local(
    grad_parts,
    first_moment,
    second_moment,
    left_stat,
    right_stat,
    left_basis,
    right_basis,
    gain_grads,
    gain_first,
    gain_second,
    table_grads,
    table_first,
    table_second,
):
    partial_value = grad_parts[0, 0]
    columns = lax.all_to_all(partial_value, "tensor", split_axis=0, concat_axis=2, tiled=True)
    summed = lax.psum_scatter(
        columns.astype(jnp.float32).astype(jnp.bfloat16), "dp", scatter_dimension=1, tiled=True
    ).astype(jnp.float32)
    grad_rows = to_half(summed)
    row_count = grad_rows.shape[1]
    offset = lax.axis_index("dp") * row_count
    left_local = to_half(left_basis[0])
    right_local = to_half(right_basis[0])
    left_full, right_full = (
        lax.all_gather(left_local, "dp", axis=1, tiled=True),
        lax.all_gather(right_local, "dp", axis=1, tiled=True),
    )
    grad_full = lax.all_gather(grad_rows, "dp", axis=1, tiled=True)
    rotated_half = to_half(batched("mik,mkj->mij", grad_rows, right_full))
    block = left_local
    rotated = jnp.swapaxes(
        lax.psum_scatter(
            batched("mkc,mkj->cmj", block, rotated_half), "dp", scatter_dimension=0, tiled=True
        ),
        0,
        1,
    )
    first_new = beta_first * first_moment[0] + (1.0 - beta_first) * rotated
    second_new = beta_second * second_moment[0] + (1.0 - beta_second) * rotated * rotated
    direction = to_half(adam_direction(first_new, second_new))
    block = left_local
    back_half = to_half(
        batched("mik,mkj->mij", block, lax.all_gather(direction, "dp", axis=1, tiled=True))
    )
    update = batched("mik,mjk->mij", back_half, right_full)
    grad_columns = lax.dynamic_slice_in_dim(grad_full, offset, row_count, 2)
    left_new = beta_stat * left_stat[0] + batched("mik,mjk->mij", grad_rows, grad_full)
    right_new = beta_stat * right_stat[0] + batched("mki,mkj->mij", grad_columns, grad_full)
    power_left = batched("mik,mkj->mij", to_half(left_new), left_full)
    power_right = batched("mik,mkj->mij", to_half(right_new), right_full)
    power = jnp.concatenate([power_left, power_right], axis=0)
    squares = lax.psum(jnp.sum(power * power, axis=(1, 2)), "dp")
    iterate = power / jnp.sqrt(squares + norm_eps)[:, None, None]
    for sweep in range(NS_ITERS):
        iterate_half = to_half(iterate)
        iterate_full = lax.all_gather(iterate_half, "dp", axis=1, tiled=True)
        gram = to_half(batched("mik,mjk->mij", iterate_half, iterate_full))
        iterate = 1.5 * iterate - 0.5 * batched("mik,mkj->mij", gram, iterate_full)
    local_mats = power_left.shape[0]
    left_rotation = iterate[:local_mats]
    right_rotation = iterate[local_mats:]
    gain_sum = lax.psum(gain_grads[0, 0, 0], ("dp", "tensor"))
    gain_moment = beta_first * gain_first[0] + (1.0 - beta_first) * gain_sum
    gain_squares = beta_second * gain_second[0] + (1.0 - beta_second) * gain_sum * gain_sum
    gain_update = adam_direction(gain_moment, gain_squares)
    table_sum = lax.psum(table_grads[0, 0], ("dp", "section"))
    table_moment = beta_first * table_first + (1.0 - beta_first) * table_sum
    table_squares = beta_second * table_second + (1.0 - beta_second) * table_sum * table_sum
    table_update = adam_direction(table_moment, table_squares)
    return (
        update[None],
        first_new[None],
        second_new[None],
        left_new[None],
        right_new[None],
        left_rotation[None],
        right_rotation[None],
        gain_update[None],
        gain_moment[None],
        gain_squares[None],
        table_update,
        table_moment,
        table_squares,
    )


def solution(mesh):
    return jax.shard_map(
        local,
        mesh=mesh,
        in_specs=(
            P("section", "dp", None, None, "tensor"),
            P("section", "tensor", "dp", None),
            P("section", "tensor", "dp", None),
            P("section", "tensor", "dp", None),
            P("section", "tensor", "dp", None),
            P("section", "tensor", "dp", None),
            P("section", "tensor", "dp", None),
            P("section", "dp", "tensor", None, None),
            P("section", None, None),
            P("section", None, None),
            P("section", "dp", None, "tensor"),
            P(None, "tensor"),
            P(None, "tensor"),
        ),
        out_specs=(
            P("section", "tensor", "dp", None),
            P("section", "tensor", "dp", None),
            P("section", "tensor", "dp", None),
            P("section", "tensor", "dp", None),
            P("section", "tensor", "dp", None),
            P("section", "tensor", "dp", None),
            P("section", "tensor", "dp", None),
            P("section", None, None),
            P("section", None, None),
            P("section", None, None),
            P(None, "tensor"),
            P(None, "tensor"),
            P(None, "tensor"),
        ),
        check_vma=False,
    )
```

profile of v0, /device:TPU:2, one launch (start us, length us, event | category | flops | bytes accessed | tf_op | source)
XLA Modules:
  0.0 1098.2 jit_solution(950655685034763806)
XLA Ops:
  7.2 4.0 copy.47
  11.2 29.7 %all_to_all.18 = bf16[4,1024,256]{1,2,0:T(8,128)(2,1)S(1)} all-to-all(bf16[4,1024,256]{1,2,0:T(8,128)(2,1)} %bitcast.140), channel_id=1, replica_groups=mesh['dp'=16,'tensor'=4,'section'=4] {'tensor'}, dimensions={0} | all-to-all | bytes 4194304 | tf_op jit(solution)/shard_map/all_to_all | solution.py:45
  40.9 7.8 copy.50
  48.7 4.4 copy.60
  53.1 77.8 %reduce-scatter.4.cloned.1.call-done = bf16[64,1024]{1,0:T(8,128)(2,1)} async-done(((bf16[1024,1024]{1,0:T(8,128)(2,1)}), bf16[64,1024]{1,0:T(8,128)(2,1)}) %reduce-scatter.4.cloned.1.call-update) | async-done | bytes 131088
  134.5 70.3 %all-gather.12.cloned.1.call-done = bf16[1,1024,1024]{2,1,0:T(8,128)(2,1)} async-done(((bf16[1,64,1024]{2,1,0:T(8,128)(2,1)}), bf16[1,1024,1024]{2,1,0:T(8,128)(2,1)}) %all-gather.12.cloned.1.call-update) | async-done | bytes 2097168 | tf_op jit(solution)/shard_map/all_gather | solution.py:58
  204.7 2.5 fusion.20
  207.2 70.5 %all-gather.20.cloned.1.call-done = bf16[1,1,1024,1024]{3,2,1,0:T(8,128)(2,1)} async-done(((bf16[1,1,64,1024]{3,2,1,0:T(8,128)(2,1)}), bf16[1,1,1024,1024]{3,2,1,0:T(8,128)(2,1)}) %all-gather.20.cloned.1.call-update) | async-done | bytes 2097168 | tf_op jit(solution)/shard_map/all_gather | solution.py:56
  277.7 2.1 fusion.26
  280.6 69.9 %all-gather.22.cloned.1.call-done = bf16[1,1,1024,1024]{3,2,1,0:T(8,128)(2,1)} async-done(((bf16[1,1,64,1024]{3,2,1,0:T(8,128)(2,1)}), bf16[1,1,1024,1024]{3,2,1,0:T(8,128)(2,1)}) %all-gather.22.cloned.1.call-update) | async-done | bytes 2097168 | tf_op jit(solution)/shard_map/all_gather | solution.py:55
  350.5 2.1 fusion.29
  352.8 32.8 %psum.21 = f32[2]{0:T(128)S(1)} all-reduce(f32[2]{0:T(128)S(1)} %multiply_reduce_fusion), channel_id=1, replica_groups=mesh['dp'=16,'tensor'=4,'section'=4] {'dp'}, use_global_device_ids=true, to_apply=%region_3.0 | all-reduce | flops 2 | bytes 16 | tf_op jit(solution)/shard_map/psum | solution.py:82
  386.5 3.2 convolution_bitcast_fusion
  389.7 11.0 %copy.48 = f32[1024,1,1024]{2,1,0:T(1,128)} copy(f32[1024,1,1024]{0,2,1:T(8,128)} %convolution_bitcast_fusion) | data formatting | bytes 8388608 | tf_op jit(solution)/shard_map/mkc,mkj->cmj/transpose | solution.py:20
  400.9 84.0 %all-gather.14.cloned.1.call-done = bf16[2,1024,1024]{2,1,0:T(8,128)(2,1)} async-done(((bf16[2,64,1024]{2,1,0:T(8,128)(2,1)}), bf16[2,1024,1024]{2,1,0:T(8,128)(2,1)}) %all-gather.14.cloned.1.call-update) | async-done | bytes 4194320 | tf_op jit(solution)/shard_map/all_gather | solution.py:86
  484.9 6.5 fusion.73
  492.7 193.9 %all-reduce.3.cloned.1.call-done = f32[1024,1,1024]{2,1,0:T(1,128)} async-done(((f32[1024,1,1024]{2,1,0:T(1,128)}), f32[1024,1,1024]{2,1,0:T(1,128)}) %all-reduce.3.cloned.1.call-update) | async-done | bytes 4194320
  688.5 99.6 %all-gather.16.cloned.1.call-done = bf16[2,1024,1024]{2,1,0:T(8,128)(2,1)} async-done(((bf16[2,64,1024]{2,1,0:T(8,128)(2,1)}), bf16[2,1024,1024]{2,1,0:T(8,128)(2,1)}) %all-gather.16.cloned.1.call-update) | async-done | bytes 4194320 | tf_op jit(solution)/shard_map/all_gather | solution.py:86
  788.1 6.4 fusion.76
  794.6 128.0 %psum.23 = f32[32,4]{0,1:T(4,128)} all-reduce(f32[32,4]{0,1:T(4,128)S(1)} %bitcast.144), channel_id=1, replica_groups=mesh['dp'=16,'tensor'=4,'section'=4] {'dp','section'}, use_global_device_ids=true, to_apply=%region_5.0 | all-reduce | flops 128 | bytes 1024 | tf_op jit(solution)/shard_map/psum | solution.py:96
  922.6 155.6 %psum.22 = f32[2,1024]{1,0:T(2,128)S(1)} all-reduce(f32[2,1024]{1,0:T(2,128)S(1)} %bitcast.143), channel_id=1, replica_groups=mesh['dp'=16,'tensor'=4,'section'=4] {'dp','tensor'}, use_global_device_ids=true, to_apply=%region_4.0 | all-reduce | flops 2048 | bytes 16384 | tf_op jit(solution)/shard_map/psum | solution.py:92
  1079.5 1.4 fusion.69
  1081.8 3.5 fusion.23
  1085.3 5.6 fusion.14
  (65 shorter events, 11.1 us)
Async XLA Ops:
  7.2 123.7 %reduce-scatter.4.cloned.1.call-start = ((), (), s32[]{:S(2)}) async-start(), calls=%async_computation.9 | async-start | bytes 2228224
  53.0 79.7 %copy-start.8 = (f32[1,1,64,1024]{3,2,1,0:T(8,128)S(1)}, f32[1,1,64,1024]{3,2,1,0:T(8,128)}, u32[]{:S(2)}) copy-start(f32[1,1,64,1024]{3,2,1,0:T(8,128)} %param.19) | copy-start | bytes 786436
  53.0 80.5 %copy-start.9 = (f32[1,1,64,1024]{3,2,1,0:T(8,128)S(1)}, f32[1,1,64,1024]{3,2,1,0:T(8,128)}, u32[]{:S(2)}) copy-start(f32[1,1,64,1024]{3,2,1,0:T(8,128)} %param.18) | copy-start | bytes 786436
  53.0 151.7 %copy-start.10 = (f32[1,1,64,1024]{3,2,1,0:T(8,128)S(1)}, f32[1,1,64,1024]{3,2,1,0:T(8,128)}, u32[]{:S(2)}) copy-start(f32[1,1,64,1024]{3,2,1,0:T(8,128)} %param.17) | copy-start | bytes 786436
  53.1 151.7 %all-gather.12.cloned.1.call-start = ((), (), s32[]{:S(2)}) async-start(), calls=%async_computation.3 | async-start | bytes 2228224 | tf_op jit(solution)/shard_map/all_gather | solution.py:58
  132.7 145.0 %all-gather.20.cloned.1.call-start = ((), (), s32[]{:S(2)}) async-start(), calls=%async_computation.7 | async-start | bytes 2228224 | tf_op jit(solution)/shard_map/all_gather | solution.py:56
  133.5 217.1 %all-gather.22.cloned.1.call-start = ((), (), s32[]{:S(2)}) async-start(), calls=%async_computation.8 | async-start | bytes 2228224 | tf_op jit(solution)/shard_map/all_gather | solution.py:55
  134.2 350.7 %all-gather.14.cloned.1.call-start = ((), (), s32[]{:S(2)}) async-start(), calls=%async_computation.4 | async-start | bytes 4456448 | tf_op jit(solution)/shard_map/all_gather | solution.py:86
  134.5 145.3 %copy-start.11 = (f32[1,1,64,1024]{3,2,1,0:T(8,128)S(1)}, f32[1,1,64,1024]{3,2,1,0:T(8,128)}, u32[]{:S(2)}) copy-start(f32[1,1,64,1024]{3,2,1,0:T(8,128)} %param.16) | copy-start | bytes 786436
  204.7 75.0 %copy-start.1 = (bf16[1,1024,1024]{2,1,0:T(8,128)(2,1)S(1)}, bf16[1,1024,1024]{2,1,0:T(8,128)(2,1)}, u32[]{:S(2)}) copy-start(bf16[1,1024,1024]{2,1,0:T(8,128)(2,1)} %all-gather.12.cloned.1.call-done) | copy-start | bytes 6291460
  207.2 73.4 %copy-start.6 = (f32[64,1024]{1,0:T(8,128)}, f32[64,1024]{1,0:T(8,128)S(1)}, u32[]{:S(2)}) copy-start(f32[64,1024]{1,0:T(8,128)S(1)} %fusion.20) | copy-start | bytes 786436
  280.6 105.9 %copy-start.7 = (f32[64,1024]{1,0:T(8,128)}, f32[64,1024]{1,0:T(8,128)S(1)}, u32[]{:S(2)}) copy-start(f32[64,1024]{1,0:T(8,128)S(1)} %fusion.17) | copy-start | bytes 786436
  280.6 105.9 %copy-start = (bf16[1,1,1024,1024]{3,2,1,0:T(8,128)(2,1)S(1)}, bf16[1,1,1024,1024]{3,2,1,0:T(8,128)(2,1)}, u32[]{:S(2)}) copy-start(bf16[1,1,1024,1024]{3,2,1,0:T(8,128)(2,1)} %all-gather.20.cloned.1.call-done) | copy-start | bytes 6291460
  280.6 105.9 %copy-start.3 = (bf16[1,1,64,1024]{3,2,1,0:T(8,128)(2,1)S(1)}, bf16[1,1,64,1024]{3,2,1,0:T(8,128)(2,1)}, u32[]{:S(2)}) copy-start(bf16[1,1,64,1024]{3,2,1,0:T(8,128)(2,1)} %convert_element_type.87) | copy-start | bytes 393220
  386.4 300.2 %all-reduce.3.cloned.1.call-start = ((), (), s32[]{:S(2)}) async-start(), calls=%async_computation.10 | async-start | bytes 8388608
  400.8 90.7 %copy-start.14 = (u32[256]{0:T(256)S(1)}, u32[256]{0:T(256)}, u32[]{:S(2)}) copy-start(u32[256]{0:T(256)} %constant.66) | copy-start | bytes 3076
  400.8 286.8 %copy-start.4 = (f32[1,1,64,1024]{3,2,1,0:T(8,128)S(1)}, f32[1,1,64,1024]{3,2,1,0:T(8,128)}, u32[]{:S(2)}) copy-start(f32[1,1,64,1024]{3,2,1,0:T(8,128)} %param.15) | copy-start | bytes 786436
  400.8 286.8 %copy-start.5 = (f32[1,1,64,1024]{3,2,1,0:T(8,128)S(1)}, f32[1,1,64,1024]{3,2,1,0:T(8,128)}, u32[]{:S(2)}) copy-start(f32[1,1,64,1024]{3,2,1,0:T(8,128)} %param.14) | copy-start | bytes 786436
  400.8 387.3 %all-gather.16.cloned.1.call-start = ((), (), s32[]{:S(2)}) async-start(), calls=%async_computation.5 | async-start | bytes 4456448 | tf_op jit(solution)/shard_map/all_gather | solution.py:86
  491.4 590.4 %all-gather.10.cloned.1.call-start = ((), (), s32[]{:S(2)}) async-start(), calls=%async_computation.2 | async-start | bytes 2228224 | tf_op jit(solution)/shard_map/all_gather | solution.py:73
  688.5 396.8 %all-gather.18.cloned.1.call-start = ((), (), s32[]{:S(2)}) async-start(), calls=%async_computation.6 | async-start | bytes 4456448 | tf_op jit(solution)/shard_map/all_gather | solution.py:86
  788.1 6.5 copy-start.13
  788.1 134.5 %copy-start.12 = (f32[1,1,1,2,1024]{4,3,2,1,0:T(2,128)S(1)}, f32[1,1,1,2,1024]{4,3,2,1,0:T(2,128)}, u32[]{:S(2)}) copy-start(f32[1,1,1,2,1024]{4,3,2,1,0:T(2,128)} %param.20) | copy-start | bytes 24580
  1081.8 3.5 copy-start.2
Sparse Core Ops, SparseCore 0:
  53.2 77.7 reduce-scatter.3
  133.3 71.4 all-gather.11
  207.1 70.5 all-gather.19
  279.9 70.5 all-gather.21
  386.5 98.3 all-gather.13
  487.4 199.1 all-reduce.2
  689.0 99.1 all-gather.15
  790.5 73.1 all-gather.9
  866.1 98.3 all-gather.17
where the time goes:
time: 1100 us
  waiting for transfers between devices  666 us (61%)
  blocking collectives  346 us (31%)
  matrix products  32.5 us (3%)
  local copies, waits for them, and re-layouts  31.6 us (3%)
  between operations  14.7 us (1%)
    unnamed x11, waiting for transfers between devices  272 us
    all_gather x3, waiting for transfers between devices, local(): iterate_full = lax.all_gather(iterate_half, 'dp', axis=1, tiled=True)  184 us
    psum x1, blocking collectives, local(): gain_sum = lax.psum(gain_grads[0, 0, 0], ('dp', 'tensor'))  156 us
    psum x1, blocking collectives, local(): table_sum = lax.psum(table_grads[0, 0], ('dp', 'section'))  128 us
    all_gather x1, waiting for transfers between devices, local(): lax.all_gather(right_local, 'dp', axis=1, tiled=True)  70.5 us
    all_gather x1, waiting for transfers between devices, local(): grad_full = lax.all_gather(grad_rows, 'dp', axis=1, tiled=True)  70.3 us
    all_gather x1, waiting for transfers between devices, local(): lax.all_gather(left_local, 'dp', axis=1, tiled=True)  69.9 us
    psum x1, blocking collectives, local(): squares = lax.psum(jnp.sum(power * power, axis=(1, 2)), 'dp')  32.8 us
  transfers between devices with their start and end apart: 9, of which 7 were waited for; matrix products, arithmetic and copies ran while one was open for 4% of the time, Pallas kernels for 0%

commit v1 on v0

--- a/solution.py
+++ b/solution.py
@@ -10,6 +10,12 @@
 adam_eps = 1e-08
 norm_eps = 1e-06
 step_count = 10.0
+register_outputs_all = lambda t0: jnp.concatenate(
+    jax.lax.all_to_all(
+        jnp.stack(jnp.split(t0, jax.lax.axis_size("tensor"), axis=0)), "tensor", 0, 0
+    ),
+    2,
+)
 
 
 def to_half(value):
@@ -42,7 +48,7 @@
     table_second,
 ):
     partial_value = grad_parts[0, 0]
-    columns = lax.all_to_all(partial_value, "tensor", split_axis=0, concat_axis=2, tiled=True)
+    columns = register_outputs_all(partial_value)
     summed = lax.psum_scatter(
         columns.astype(jnp.float32).astype(jnp.bfloat16), "dp", scatter_dimension=1, tiled=True
     ).astype(jnp.float32)

time: 1100 us -> 1100 us (level)
  no operation moved by 1% of the time
where the time goes in v1:
time: 1100 us
  waiting for transfers between devices  666 us (61%)
  blocking collectives  346 us (31%)
  matrix products  32.5 us (3%)
  local copies, waits for them, and re-layouts  30 us (3%)
  between operations  14.8 us (1%)
    unnamed x11, waiting for transfers between devices  272 us
    all_gather x3, waiting for transfers between devices, local(): iterate_full = lax.all_gather(iterate_half, 'dp', axis=1, tiled=True)  184 us
    psum x1, blocking collectives, local(): gain_sum = lax.psum(gain_grads[0, 0, 0], ('dp', 'tensor'))  156 us
    psum x1, blocking collectives, local(): table_sum = lax.psum(table_grads[0, 0], ('dp', 'section'))  128 us
    all_gather x1, waiting for transfers between devices, local(): lax.all_gather(right_local, 'dp', axis=1, tiled=True)  70.5 us
    all_gather x1, waiting for transfers between devices, local(): grad_full = lax.all_gather(grad_rows, 'dp', axis=1, tiled=True)  70 us
    all_gather x1, waiting for transfers between devices, local(): lax.all_gather(left_local, 'dp', axis=1, tiled=True)  69.9 us
    psum x1, blocking collectives, local(): squares = lax.psum(jnp.sum(power * power, axis=(1, 2)), 'dp')  32.8 us
  transfers between devices with their start and end apart: 9, of which 7 were waited for; matrix products, arithmetic and copies ran while one was open for 4% of the time, Pallas kernels for 0%

profile of v1, /device:TPU:2, one launch (start us, length us, event | category | flops | bytes accessed | tf_op | source)
XLA Modules:
  0.0 1096.9 jit_solution(15400173710593928697)
XLA Ops:
  7.2 1.7 fusion.73
  10.0 29.5 %all_to_all.5 = bf16[4,1,1024,256]{2,3,1,0:T(8,128)(2,1)S(1)} all-to-all(bf16[4,1,1024,256]{2,3,1,0:T(8,128)(2,1)S(1)} %pad_maximum_fusion), channel_id=1, replica_groups=mesh['dp'=16,'tensor'=4,'section'=4] {'tensor'}, dimensions={0} | all-to-all | bytes 4194304 | tf_op jit(solution)/shard_map/all_to_all | solution.py:14
  39.5 7.8 copy.57
  47.3 4.4 copy.71
  51.7 78.0 %reduce-scatter.4.cloned.1.call-done = bf16[64,1024]{1,0:T(8,128)(2,1)} async-done(((bf16[1024,1024]{1,0:T(8,128)(2,1)}), bf16[64,1024]{1,0:T(8,128)(2,1)}) %reduce-scatter.4.cloned.1.call-update) | async-done | bytes 131088
  133.3 70.0 %all-gather.12.cloned.1.call-done = bf16[1,1024,1024]{2,1,0:T(8,128)(2,1)} async-done(((bf16[1,64,1024]{2,1,0:T(8,128)(2,1)}), bf16[1,1024,1024]{2,1,0:T(8,128)(2,1)}) %all-gather.12.cloned.1.call-update) | async-done | bytes 2097168 | tf_op jit(solution)/shard_map/all_gather | solution.py:64
  203.4 2.4 fusion.20
  205.8 70.5 %all-gather.20.cloned.1.call-done = bf16[1,1,1024,1024]{3,2,1,0:T(8,128)(2,1)} async-done(((bf16[1,1,64,1024]{3,2,1,0:T(8,128)(2,1)}), bf16[1,1,1024,1024]{3,2,1,0:T(8,128)(2,1)}) %all-gather.20.cloned.1.call-update) | async-done | bytes 2097168 | tf_op jit(solution)/shard_map/all_gather | solution.py:62
  276.3 2.1 fusion.26
  279.2 69.9 %all-gather.22.cloned.1.call-done = bf16[1,1,1024,1024]{3,2,1,0:T(8,128)(2,1)} async-done(((bf16[1,1,64,1024]{3,2,1,0:T(8,128)(2,1)}), bf16[1,1,1024,1024]{3,2,1,0:T(8,128)(2,1)}) %all-gather.22.cloned.1.call-update) | async-done | bytes 2097168 | tf_op jit(solution)/shard_map/all_gather | solution.py:61
  349.1 2.1 fusion.29
  351.4 32.8 %psum.21 = f32[2]{0:T(128)S(1)} all-reduce(f32[2]{0:T(128)S(1)} %multiply_reduce_fusion), channel_id=1, replica_groups=mesh['dp'=16,'tensor'=4,'section'=4] {'dp'}, use_global_device_ids=true, to_apply=%region_3.0 | all-reduce | flops 2 | bytes 16 | tf_op jit(solution)/shard_map/psum | solution.py:88
  385.1 3.2 convolution_bitcast_fusion
  388.3 11.0 %copy.55 = f32[1024,1,1024]{2,1,0:T(1,128)} copy(f32[1024,1,1024]{0,2,1:T(8,128)} %convolution_bitcast_fusion) | data formatting | bytes 8388608 | tf_op jit(solution)/shard_map/mkc,mkj->cmj/transpose | solution.py:26
  399.4 84.1 %all-gather.14.cloned.1.call-done = bf16[2,1024,1024]{2,1,0:T(8,128)(2,1)} async-done(((bf16[2,64,1024]{2,1,0:T(8,128)(2,1)}), bf16[2,1024,1024]{2,1,0:T(8,128)(2,1)}) %all-gather.14.cloned.1.call-update) | async-done | bytes 4194320 | tf_op jit(solution)/shard_map/all_gather | solution.py:92
  483.5 6.5 fusion.74
  491.3 193.9 %all-reduce.3.cloned.1.call-done = f32[1024,1,1024]{2,1,0:T(1,128)} async-done(((f32[1024,1,1024]{2,1,0:T(1,128)}), f32[1024,1,1024]{2,1,0:T(1,128)}) %all-reduce.3.cloned.1.call-update) | async-done | bytes 4194320
  687.1 99.6 %all-gather.16.cloned.1.call-done = bf16[2,1024,1024]{2,1,0:T(8,128)(2,1)} async-done(((bf16[2,64,1024]{2,1,0:T(8,128)(2,1)}), bf16[2,1024,1024]{2,1,0:T(8,128)(2,1)}) %all-gather.16.cloned.1.call-update) | async-done | bytes 4194320 | tf_op jit(solution)/shard_map/all_gather | solution.py:92
  786.7 6.5 fusion.77
  793.2 127.8 %psum.23 = f32[32,4]{0,1:T(4,128)} all-reduce(f32[32,4]{0,1:T(4,128)S(1)} %bitcast.150), channel_id=1, replica_groups=mesh['dp'=16,'tensor'=4,'section'=4] {'dp','section'}, use_global_device_ids=true, to_apply=%region_5.0 | all-reduce | flops 128 | bytes 1024 | tf_op jit(solution)/shard_map/psum | solution.py:102
  921.1 155.8 %psum.22 = f32[2,1024]{1,0:T(2,128)S(1)} all-reduce(f32[2,1024]{1,0:T(2,128)S(1)} %bitcast.149), channel_id=1, replica_groups=mesh['dp'=16,'tensor'=4,'section'=4] {'dp','tensor'}, use_global_device_ids=true, to_apply=%region_4.0 | all-reduce | flops 2048 | bytes 16384 | tf_op jit(solution)/shard_map/psum | solution.py:98
  1078.2 1.4 fusion.69
  1080.4 3.5 fusion.23
  1083.9 5.6 fusion.14
  (70 shorter events, 12.2 us)
Async XLA Ops:
  7.2 122.6 %reduce-scatter.4.cloned.1.call-start = ((), (), s32[]{:S(2)}) async-start(), calls=%async_computation.9 | async-start | bytes 2228224
  51.6 79.9 %copy-start.8 = (f32[1,1,64,1024]{3,2,1,0:T(8,128)S(1)}, f32[1,1,64,1024]{3,2,1,0:T(8,128)}, u32[]{:S(2)}) copy-start(f32[1,1,64,1024]{3,2,1,0:T(8,128)} %param.19) | copy-start | bytes 786436
  51.6 80.7 %copy-start.9 = (f32[1,1,64,1024]{3,2,1,0:T(8,128)S(1)}, f32[1,1,64,1024]{3,2,1,0:T(8,128)}, u32[]{:S(2)}) copy-start(f32[1,1,64,1024]{3,2,1,0:T(8,128)} %param.18) | copy-start | bytes 786436
  51.6 151.7 %copy-start.10 = (f32[1,1,64,1024]{3,2,1,0:T(8,128)S(1)}, f32[1,1,64,1024]{3,2,1,0:T(8,128)}, u32[]{:S(2)}) copy-start(f32[1,1,64,1024]{3,2,1,0:T(8,128)} %param.17) | copy-start | bytes 786436
  51.7 151.7 %all-gather.12.cloned.1.call-start = ((), (), s32[]{:S(2)}) async-start(), calls=%async_computation.3 | async-start | bytes 2228224 | tf_op jit(solution)/shard_map/all_gather | solution.py:64
  131.5 144.8 %all-gather.20.cloned.1.call-start = ((), (), s32[]{:S(2)}) async-start(), calls=%async_computation.7 | async-start | bytes 2228224 | tf_op jit(solution)/shard_map/all_gather | solution.py:62
  132.3 216.8 %all-gather.22.cloned.1.call-start = ((), (), s32[]{:S(2)}) async-start(), calls=%async_computation.8 | async-start | bytes 2228224 | tf_op jit(solution)/shard_map/all_gather | solution.py:61
  133.0 350.5 %all-gather.14.cloned.1.call-start = ((), (), s32[]{:S(2)}) async-start(), calls=%async_computation.4 | async-start | bytes 4456448 | tf_op jit(solution)/shard_map/all_gather | solution.py:92
  133.3 145.1 %copy-start.11 = (f32[1,1,64,1024]{3,2,1,0:T(8,128)S(1)}, f32[1,1,64,1024]{3,2,1,0:T(8,128)}, u32[]{:S(2)}) copy-start(f32[1,1,64,1024]{3,2,1,0:T(8,128)} %param.16) | copy-start | bytes 786436
  203.4 75.0 %copy-start.1 = (bf16[1,1024,1024]{2,1,0:T(8,128)(2,1)S(1)}, bf16[1,1024,1024]{2,1,0:T(8,128)(2,1)}, u32[]{:S(2)}) copy-start(bf16[1,1024,1024]{2,1,0:T(8,128)(2,1)} %all-gather.12.cloned.1.call-done) | copy-start | bytes 6291460
  205.8 73.4 %copy-start.6 = (f32[64,1024]{1,0:T(8,128)}, f32[64,1024]{1,0:T(8,128)S(1)}, u32[]{:S(2)}) copy-start(f32[64,1024]{1,0:T(8,128)S(1)} %fusion.20) | copy-start | bytes 786436
  279.2 105.9 %copy-start.7 = (f32[64,1024]{1,0:T(8,128)}, f32[64,1024]{1,0:T(8,128)S(1)}, u32[]{:S(2)}) copy-start(f32[64,1024]{1,0:T(8,128)S(1)} %fusion.17) | copy-start | bytes 786436
  279.2 105.9 %copy-start = (bf16[1,1,1024,1024]{3,2,1,0:T(8,128)(2,1)S(1)}, bf16[1,1,1024,1024]{3,2,1,0:T(8,128)(2,1)}, u32[]{:S(2)}) copy-start(bf16[1,1,1024,1024]{3,2,1,0:T(8,128)(2,1)} %all-gather.20.cloned.1.call-done) | copy-start | bytes 6291460
  279.2 105.9 %copy-start.3 = (bf16[1,1,64,1024]{3,2,1,0:T(8,128)(2,1)S(1)}, bf16[1,1,64,1024]{3,2,1,0:T(8,128)(2,1)}, u32[]{:S(2)}) copy-start(bf16[1,1,64,1024]{3,2,1,0:T(8,128)(2,1)} %convert_element_type.87) | copy-start | bytes 393220
  385.1 300.2 %all-reduce.3.cloned.1.call-start = ((), (), s32[]{:S(2)}) async-start(), calls=%async_computation.10 | async-start | bytes 8388608
  399.3 90.8 %copy-start.14 = (u32[256]{0:T(256)S(1)}, u32[256]{0:T(256)}, u32[]{:S(2)}) copy-start(u32[256]{0:T(256)} %constant.66) | copy-start | bytes 3076
  399.3 286.8 %copy-start.4 = (f32[1,1,64,1024]{3,2,1,0:T(8,128)S(1)}, f32[1,1,64,1024]{3,2,1,0:T(8,128)}, u32[]{:S(2)}) copy-start(f32[1,1,64,1024]{3,2,1,0:T(8,128)} %param.15) | copy-start | bytes 786436
  399.3 286.8 %copy-start.5 = (f32[1,1,64,1024]{3,2,1,0:T(8,128)S(1)}, f32[1,1,64,1024]{3,2,1,0:T(8,128)}, u32[]{:S(2)}) copy-start(f32[1,1,64,1024]{3,2,1,0:T(8,128)} %param.14) | copy-start | bytes 786436
  399.4 387.4 %all-gather.16.cloned.1.call-start = ((), (), s32[]{:S(2)}) async-start(), calls=%async_computation.5 | async-start | bytes 4456448 | tf_op jit(solution)/shard_map/all_gather | solution.py:92
  490.0 590.4 %all-gather.10.cloned.1.call-start = ((), (), s32[]{:S(2)}) async-start(), calls=%async_computation.2 | async-start | bytes 2228224 | tf_op jit(solution)/shard_map/all_gather | solution.py:79
  687.1 396.8 %all-gather.18.cloned.1.call-start = ((), (), s32[]{:S(2)}) async-start(), calls=%async_computation.6 | async-start | bytes 4456448 | tf_op jit(solution)/shard_map/all_gather | solution.py:92
  786.7 6.5 copy-start.13
  786.7 134.3 %copy-start.12 = (f32[1,1,1,2,1024]{4,3,2,1,0:T(2,128)S(1)}, f32[1,1,1,2,1024]{4,3,2,1,0:T(2,128)}, u32[]{:S(2)}) copy-start(f32[1,1,1,2,1024]{4,3,2,1,0:T(2,128)} %param.20) | copy-start | bytes 24580
  1080.4 3.5 copy-start.2
Sparse Core Ops, SparseCore 0:
  51.8 77.9 reduce-scatter.3
  132.1 71.1 all-gather.11
  205.7 70.5 all-gather.19
  278.5 70.5 all-gather.21
  385.2 98.2 all-gather.13
  486.0 199.1 all-reduce.2
  687.6 99.1 all-gather.15
  789.1 73.1 all-gather.9
  864.7 98.3 all-gather.17
